TPU v7x, 128 devices: a whole 4x4x4 slice. The times are simulated.
128 devices in a mesh: gy: 16 (over z_hi, x, core), gz: 8 (over z_lo, y).
Axes of the slice: x: 4, y: 4, z: 4 (z_hi: 2, z_lo: 2; z = z_hi * 2 + z_lo), core: 2. Of those that a mesh axis runs over, the one named last changes fastest.
Arguments:
- reference_image: bfloat16 [64, 1024, 4096], P(None, 'gy', 'gz'), may hold values from -6 to 6
- deformed: bfloat16 [64, 1024, 4096], P(None, 'gy', 'gz'), may hold values from -12 to 12
- displacement: bfloat16 [3, 64, 1024, 4096], P(None, None, 'gy', 'gz'), may hold values from -1 to 1
- plane_factors: float32 [2, 32, 8, 128], P(None, None, None, 'gy'), may hold values from -2.5 to 2.5
- depth_factors: float32 [2, 32, 4096], P(None, None, 'gz'), may hold values from -6 to 6
Outputs:
- residual: bfloat16 [64, 1024, 4096], P(None, 'gy', 'gz')
- step_plane: float32 [2, 32, 8, 128], P(None, None, None, 'gy')
- step_depth: float32 [2, 32, 4096], P(None, None, 'gz')
All inputs are finite; a program needn't handle non-finite values.
Results may differ from a plain program's by a relative error of at most 0.0004.
Values may be sent and summed in bfloat16 or wider, within the bound.
A program may use at most 256 MiB of HBM per device.

v0:
```python
import jax
import jax.numpy as jnp
from jax import lax
from jax.sharding import PartitionSpec as P

RANK = 32
KNOT = 8
epsilon = 1e-06
damping = 0.01
highest = lax.Precision.HIGHEST


def extended(cells, sides, width):
    for axis, dim in sides:
        count = lax.axis_size(axis)
        ends = count - 1
        head = lax.slice_in_dim(cells, 0, width, axis=dim)
        tail = lax.slice_in_dim(cells, cells.shape[dim] - width, cells.shape[dim], axis=dim)
        cells = jnp.concatenate(
            [
                lax.ppermute(tail, axis, [(i, (i + 1) % count) for i in range(ends)]),
                cells,
                lax.ppermute(head, axis, [((i + 1) % count, i) for i in range(ends)]),
            ],
            axis=dim,
        )
    return cells


def tent_weights(shift):
    moved = shift.astype(jnp.float32)
    return [jnp.maximum(0.0, 1.0 - jnp.abs(moved - offset)) for offset in (-1.0, 0.0, 1.0)]


def warp_image(padded, displacement):
    depth_x, width_y, width_z = displacement.shape[1:]
    weight_x = tent_weights(displacement[0])
    weight_y = tent_weights(displacement[1])
    weight_z = tent_weights(displacement[2])
    summed = jnp.zeros((depth_x, width_y, width_z), jnp.float32)
    for along_x in range(3):
        for along_y in range(3):
            partial_z = jnp.zeros((depth_x, width_y, width_z), jnp.float32)
            for along_z in range(3):
                window = padded[
                    along_x : along_x + depth_x,
                    along_y : along_y + width_y,
                    along_z : along_z + width_z,
                ]
                partial_z = partial_z + weight_z[along_z] * window.astype(jnp.float32)
            summed = summed + weight_x[along_x] * weight_y[along_y] * partial_z
    return summed


def expand_nodes(nodes):
    return jnp.repeat(jnp.repeat(nodes, KNOT, axis=2), KNOT, axis=3)


def reduce_nodes(field):
    leading = field.shape[:-2]
    depth_x, width_y = field.shape[-2:]
    shaped = field.reshape(leading + (depth_x // KNOT, KNOT, width_y // KNOT, KNOT))
    return jnp.sum(shaped, axis=(-3, -1))


def contract_rank(left, right):
    return lax.dot_general(left, right, (((0,), (0,)), ((), ())), precision=highest)


def contract_cells(left, right):
    return jnp.dot(left, right, precision=highest)


def contract_depth(left, right):
    return lax.dot_general(left, right, (((1,), (1,)), ((), ())), precision=highest)


def strip_terms(image, padded, displacement, plane_voxels, depth_factors):
    depth_x, width_y, width_z = image.shape
    cells = depth_x * width_y
    warped = warp_image(padded, displacement).reshape(cells, width_z)
    values = image.astype(jnp.float32).reshape(cells, width_z)
    flat_plane = plane_voxels.reshape(2, plane_voxels.shape[1], cells)
    contrast = contract_rank(flat_plane[0], depth_factors[0])
    brightness = contract_rank(flat_plane[1], depth_factors[1])
    misfit = warped - contrast * values - brightness
    product = misfit * values
    squares = values * values
    grad_depth = -jnp.stack(
        [contract_cells(flat_plane[0], product), contract_cells(flat_plane[1], misfit)]
    )
    level_sum = jnp.sum(flat_plane[1] * flat_plane[1], axis=1)
    first_depth = contract_cells(flat_plane[0] * flat_plane[0], squares)
    grad_voxels = -jnp.stack(
        [contract_depth(depth_factors[0], product), contract_depth(depth_factors[1], misfit)]
    )
    diag_voxels = contract_depth(depth_factors[0] * depth_factors[0], squares)
    grad_plane = reduce_nodes(grad_voxels.reshape(2, -1, depth_x, width_y))
    first_diag = reduce_nodes(diag_voxels.reshape(-1, depth_x, width_y))
    depth_level = KNOT * KNOT * jnp.sum(depth_factors[1] * depth_factors[1], axis=1)
    squared_sum = jnp.sum(misfit * misfit)
    residual = misfit.reshape(depth_x, width_y, width_z).astype(jnp.bfloat16)
    return (
        residual,
        squared_sum,
        grad_plane,
        first_diag,
        depth_level,
        grad_depth,
        first_depth,
        level_sum,
    )


def local(reference_image, deformed, displacement, plane_factors, depth_factors):
    rimmed = extended(deformed, (("gy", 1), ("gz", 2)), 1)
    padded = jnp.pad(rimmed, ((1, 1), (0, 0), (0, 0)))
    plane_voxels = expand_nodes(plane_factors)
    (
        residual,
        local_energy,
        grad_plane,
        first_diag,
        depth_level,
        grad_depth,
        first_depth,
        level_sum,
    ) = strip_terms(reference_image, padded, displacement, plane_voxels, depth_factors)
    nodes_x = plane_factors.shape[2]
    nodes_y = plane_factors.shape[3] * lax.axis_size("gy")
    full_z = depth_factors.shape[2] * lax.axis_size("gz")
    energy = lax.psum(local_energy, ("gy", "gz"))
    grad_plane, first_diag, depth_level = lax.psum((grad_plane, first_diag, depth_level), "gz")
    diag_plane = jnp.stack(
        [first_diag, jnp.broadcast_to(depth_level[:, None, None], first_diag.shape)]
    )
    lam_plane = damping * RANK * energy / (nodes_x * nodes_y)
    lam_depth = damping * energy / full_z
    step_plane = -grad_plane / (diag_plane + lam_plane + epsilon)
    grad_depth, first_depth, level_sum = lax.psum((grad_depth, first_depth, level_sum), "gy")
    diag_depth = jnp.stack([first_depth, jnp.broadcast_to(level_sum[:, None], first_depth.shape)])
    step_depth = -grad_depth / (diag_depth + lam_depth + epsilon)
    return (residual, step_plane, step_depth)


def solution(mesh):
    placed = (
        P(None, "gy", "gz"),
        P(None, "gy", "gz"),
        P(None, None, "gy", "gz"),
        P(None, None, None, "gy"),
        P(None, None, "gz"),
    )
    return jax.shard_map(
        local,
        mesh=mesh,
        in_specs=placed,
        out_specs=(P(None, "gy", "gz"), P(None, None, None, "gy"), P(None, None, "gz")),
        check_vma=False,
    )
```

profile of v0, /device:TPU:7, one launch (start us, length us, event | category | flops | bytes accessed | tf_op | source)
XLA Modules:
  0.0 613.2 jit_solution(7184010167852653225)
XLA Ops:
  7.2 0.0 copy-start.7
  7.2 0.0 copy-start.5
  7.2 0.0 all-reduce.5.cloned.1.call-start
  7.2 1.4 fusion.133
  8.7 6.0 collective-permute-start
  14.7 0.0 copy-start.4
  14.7 2.2 collective-permute-start.1
  16.9 9.0 %fusion.132 = (bf16[1,64,64,512]{3,2,1,0:T(8,128)(2,1)}, bf16[1,64,64,512]{3,2,1,0:T(8,128)(2,1)}, bf16[1,64,64,512]{3,2,1,0:T(8,128)(2,1)}) fusion(bf16[3,64,64,512]{3,2,1,0:T(8,128)(2,1)} %param.7), kind=kLoop, calls=%fused_computation.173 | loop fusion | bytes 25165824 | tf_op jit(solution)/shard_map/slice | solution.py:39
  25.9 0.0 copy-done.7
  25.9 0.0 copy-done.5
  25.9 0.1 fusion.122
  26.1 0.3 broadcast_in_dim.28
  26.4 0.0 copy-start.1
  26.4 8.8 %fusion.124 = f32[4096,512]{1,0:T(8,128)} fusion(f32[32,4096]{0,1:T(8,128)S(1)} %bitcast.293, f32[2,32,512]{2,1,0:T(8,128)S(1)} %copy-done.5), kind=kOutput, calls=%fused_computation.159 | convolution fusion | flops 805306368 | bytes 10551296 | tf_op jit(solution)/shard_map/dot_general | solution.py:67
  35.1 0.0 copy-done.1
  35.2 0.0 copy-done.4
  35.2 1.2 convert_multiply_fusion
  36.5 7.4 %convolution_reduce_fusion = f32[32,8,8]{0,2,1:T(8,128)} fusion(f32[8,8,8,8,512]{4,3,2,1,0:T(8,128)S(1)} %bitcast.291, f32[2,32,512]{2,1,0:T(8,128)S(1)} %copy-done.5), kind=kOutput, calls=%fused_computation.139 | convolution fusion | flops 805451776 | bytes 8462336 | tf_op jit(solution)/shard_map/dot_general | solution.py:75
  43.9 0.3 broadcast_in_dim.34
  44.2 5.7 convolution_bitcast_fusion.2
  49.8 0.5 broadcast_multiply_fusion
  50.4 13.0 %copy.49 = bf16[64,64,512]{1,0,2:T(8,128)(2,1)} copy(bf16[64,64,512]{2,1,0:T(8,128)(2,1)} %param.6) | data formatting | bytes 8388608 | tf_op args[1]
  63.4 0.2 copy.59
  63.5 0.0 collective-permute-done
  63.5 12.7 %copy.48 = bf16[64,1,512]{1,0,2:T(8,128)(2,1)} copy(bf16[64,1,512]{2,0,1:T(8,128)(2,1)S(1)} %collective-permute-done) | data formatting | bytes 131072 | tf_op jit(solution)/shard_map/ppermute | solution.py:21
  76.2 0.0 collective-permute-done.1
  76.2 12.7 %copy.50 = bf16[64,1,512]{1,0,2:T(8,128)(2,1)} copy(bf16[64,1,512]{2,0,1:T(8,128)(2,1)S(1)} %collective-permute-done.1) | data formatting | bytes 131072 | tf_op jit(solution)/shard_map/ppermute | solution.py:23
  88.9 0.9 pad_maximum_fusion.5
  89.8 3.2 collective-permute-start.2
  93.0 1.3 collective-permute-start.3
  94.3 0.3 broadcast_reduce_fusion
  94.6 13.4 %copy.61 = bf16[1,64,64,512]{2,1,3,0:T(8,128)(2,1)} copy(bf16[1,64,64,512]{3,2,1,0:T(8,128)(2,1)} %get-tuple-element.14) | data formatting | bytes 8388608
  108.0 13.0 %copy.62 = bf16[1,64,64,512]{2,1,3,0:T(8,128)(2,1)} copy(bf16[1,64,64,512]{3,2,1,0:T(8,128)(2,1)} %get-tuple-element.13) | data formatting | bytes 8388608
  121.0 12.9 %copy.63 = bf16[1,64,64,512]{2,1,3,0:T(8,128)(2,1)} copy(bf16[1,64,64,512]{3,2,1,0:T(8,128)(2,1)} %get-tuple-element.12) | data formatting | bytes 8388608
  133.9 32.9 %psum.55 = f32[32]{0:T(128)S(1)} all-reduce(f32[32]{0:T(128)S(1)} %broadcast_reduce_fusion), channel_id=1, replica_groups=mesh['gy'=16,'gz'=8] {'gy'}, use_global_device_ids=true, to_apply=%region_11.12 | all-reduce | flops 32 | bytes 256 | tf_op jit(solution)/shard_map/psum | solution.py:140
  166.8 0.0 collective-permute-done.2
  166.8 0.0 collective-permute-done.3
  166.8 24.1 %maximum_maximum_fusion = (bf16[64,66,513]{1,0,2:T(8,128)(2,1)S(1)}, bf16[64,66,513]{1,0,2:T(8,128)(2,1)}) fusion(bf16[64,1,512]{1,0,2:T(8,128)(2,1)} %copy.50, bf16[64,64,512]{1,0,2:T(8,128)(2,1)} %copy.49, bf16[64,1,512]{1,0,2:T(8,128)(2,1)} %copy.48, bf16[64,66,1]{1,0,2:T(8,128)(2,1)S(1)} %collective-permute-done.2, ...), kind=kLoop, calls=%fused_computation.126 | loop fusion | flops 34670592 | bytes 13009920 | tf_op jit(solution)/shard_map/concatenate | solution.py:19
  190.8 24.0 %select_maximum_fusion = bf16[66,66,514]{1,0,2:T(8,128)(2,1)S(1)} fusion(bf16[64,66,1]{1,0,2:T(8,128)(2,1)S(1)} %collective-permute-done.3, bf16[64,66,1]{1,0,2:T(8,128)(2,1)S(1)} %collective-permute-done.2, bf16[64,1,512]{1,0,2:T(8,128)(2,1)} %copy.50, bf16[64,64,512]{1,0,2:T(8,128)(2,1)} %copy.49, bf16[64,1,512]{1,0,2:T(8,128)(2,1)} %copy.48), kind=kLoop, calls=%fused_computation.119 | loop fusion | flops 40301712 | bytes 8820240 | tf_op jit(solution)/shard_map/concatenate | solution.py:19
  214.8 119.0 %fusion.15 = f32[64,64,512]{1,0,2:T(8,128)} fusion(bf16[1,64,64,512]{2,1,3,0:T(8,128)(2,1)} %copy.61, bf16[1,64,64,512]{2,1,3,0:T(8,128)(2,1)} %copy.62, bf16[1,64,64,512]{2,1,3,0:T(8,128)(2,1)} %copy.63, bf16[64,64,512]{1,0,2:T(8,128)(2,1)} %copy.49, bf16[66,66,514]{1,0,2:T(8,128)(2,1)S(1)} %select_maximum_fusion, ...), kind=kLoop, calls=%fused_computation.26 | loop fusion | flops 293601280 | bytes 125960192 | tf_op jit(solution)/shard_map/add | solution.py:51
  333.9 12.7 %copy.56 = f32[64,64,512]{2,1,0:T(8,128)} copy(f32[64,64,512]{1,0,2:T(8,128)} %fusion.15) | data formatting | bytes 16777216 | tf_op jit(solution)/shard_map/add | solution.py:51
  346.6 1.6 broadcast_in_dim.32
  348.3 17.3 %multiply_reduce_fusion = (f32[]{:T(128)}, f32[4096,512]{1,0:T(8,128)}, bf16[4096,512]{1,0:T(8,128)(2,1)}, f32[4096,512]{1,0:T(8,128)S(1)}) fusion(bf16[64,64,512]{2,1,0:T(8,128)(2,1)} %param.5, f32[32,4096]{0,1:T(8,128)} %bitcast.295, f32[2,32,512]{2,1,0:T(8,128)S(1)} %copy-done.5, f32[4096,512]{1,0:T(8,128)} %fusion.124, f32[64,64,512]{2,1,0:T(8,128)} %copy.56), kind=kOutput, calls=%fused_computation.135 | convolution fusion | flops 822083584 | bytes 42532868 | tf_op jit(solution)/shard_map/dot_general | solution.py:67
  365.6 0.0 copy-done.2
  365.6 10.2 %convolution_bitcast_fusion.4 = f32[1,32,512]{2,1,0:T(8,128)S(1)} fusion(f32[4096,512]{1,0:T(8,128)} %get-tuple-element.16, f32[32,4096]{0,1:T(8,128)S(1)} %bitcast.294), kind=kOutput, calls=%fused_computation.142 | convolution fusion | flops 805306368 | bytes 8978432 | tf_op jit(solution)/shard_map/dot_general | solution.py:71
  375.8 0.0 copy-done
  375.8 7.7 %convolution_bitcast_fusion.1 = f32[32,4096]{1,0:T(8,128)S(1)} fusion(f32[4096,512]{1,0:T(8,128)S(1)} %copy-done, f32[2,32,512]{2,1,0:T(8,128)S(1)} %copy-done.5), kind=kOutput, calls=%fused_computation.137 | convolution fusion | flops 805306368 | bytes 8978432 | tf_op jit(solution)/shard_map/dot_general | solution.py:75
  383.5 0.0 copy-done.3
  383.5 0.0 copy-start.6
  383.5 0.0 copy-start.8
  383.6 5.3 convolution_bitcast_fusion.3
  388.8 8.0 %convolution_bitcast_fusion = f32[32,4096]{1,0:T(8,128)S(1)} fusion(f32[4096,512]{1,0:T(8,128)S(1)} %get-tuple-element.22, f32[2,32,512]{2,1,0:T(8,128)S(1)} %copy-done.5), kind=kOutput, calls=%fused_computation.136 | convolution fusion | flops 805306368 | bytes 8978432 | tf_op jit(solution)/shard_map/dot_general | solution.py:75
  396.8 68.7 %psum.52 = f32[]{:T(128)} all-reduce(f32[]{:T(128)} %get-tuple-element.15), channel_id=1, replica_groups=mesh['gy'=16,'gz'=8] {'gy','gz'}, use_global_device_ids=true, to_apply=%region_7.8 | all-reduce | flops 1 | bytes 8 | tf_op jit(solution)/shard_map/psum | solution.py:132
  465.5 0.6 copy.57
  466.1 2.0 copy.58
  468.1 2.2 maximum_reduce_fusion
  471.6 0.7 maximum_negate_fusion
  472.3 0.0 all-reduce.5.cloned.1.call-update
  472.3 0.0 copy-done.6
  472.3 26.1 %all-reduce.2 = (f32[32]{0:T(128)S(1)}, f32[1,32,8,8]{1,3,2,0:T(8,128)S(1)}, f32[2,32,8,8]{1,3,2,0:T(8,128)S(1)}) all-reduce(f32[32]{0:T(128)S(1)} %copy-done.8, f32[1,32,8,8]{1,3,2,0:T(8,128)S(1)} %bitcast.303, f32[2,32,8,8]{1,3,2,0:T(8,128)S(1)} %neg.13), channel_id=1, replica_groups=mesh['gy'=16,'gz'=8] {'gz'}, use_global_device_ids=true, to_apply=%region_5.6 | all-reduce | flops 6176 | bytes 49408 | tf_op jit(solution)/shard_map/psum | solution.py:133
  498.4 0.7 fusion.118
  499.1 105.1 %all-reduce.5.cloned.1.call-done = (f32[1,32,512]{2,1,0:T(8,128)}, f32[2,32,512]{2,1,0:T(8,128)}) async-done(((f32[1,32,512]{2,1,0:T(8,128)}, f32[2,32,512]{2,1,0:T(8,128)}), (f32[1,32,512]{2,1,0:T(8,128)}, f32[2,32,512]{2,1,0:T(8,128)})) %all-reduce.5.cloned.1.call-update) | async-done | bytes 196624 | tf_op jit(solution)/shard_map/psum | solution.py:140
  604.2 0.1 stack_broadcast_in_dim.5
  604.2 1.6 fusion.116
  (12 shorter events, 0.1 us)
Async XLA Ops:
  7.2 18.8 %copy-start.7 = (f32[2,32,8,8]{1,3,2,0:T(8,128)S(1)}, f32[2,32,8,8]{1,3,2,0:T(8,128)}, u32[]{:S(2)}) copy-start(f32[2,32,8,8]{1,3,2,0:T(8,128)} %param.8) | copy-start | bytes 49156
  7.2 18.8 %copy-start.5 = (f32[2,32,512]{2,1,0:T(8,128)S(1)}, f32[2,32,512]{2,1,0:T(8,128)}, u32[]{:S(2)}) copy-start(f32[2,32,512]{2,1,0:T(8,128)} %param.9) | copy-start | bytes 393220
  7.2 597.0 %all-reduce.5.cloned.1.call-start = ((), (), s32[]{:S(2)}) async-start(), calls=%async_computation | async-start | bytes 393216 | tf_op jit(solution)/shard_map/psum | solution.py:140
  8.7 54.8 %collective-permute-start = (bf16[64,1,512]{2,0,1:T(8,128)(2,1)S(1)}, bf16[64,1,512]{2,0,1:T(8,128)(2,1)S(1)}, u32[]{:S(2)}, u32[]{:S(2)}) collective-permute-start(bf16[64,1,512]{2,0,1:T(8,128)(2,1)S(1)} %copy.64), channel_id=1, source_target_pairs={{0,8},{8,16},{16,24},{24,32},{32,40},{40,48},{48,56},{56,64},{64,7... | collective-permute-start | bytes 196616 | tf_op jit(solution)/shard_map/ppermute | solution.py:21
  14.7 20.5 %copy-start.4 = (bf16[64,64,512]{2,1,0:T(8,128)(2,1)S(1)}, bf16[64,64,512]{2,1,0:T(8,128)(2,1)}, u32[]{:S(2)}) copy-start(bf16[64,64,512]{2,1,0:T(8,128)(2,1)} %param.5) | copy-start | bytes 12582916
  14.7 61.5 %collective-permute-start.1 = (bf16[64,1,512]{2,0,1:T(8,128)(2,1)S(1)}, bf16[64,1,512]{2,0,1:T(8,128)(2,1)S(1)}, u32[]{:S(2)}, u32[]{:S(2)}) collective-permute-start(bf16[64,1,512]{2,0,1:T(8,128)(2,1)S(1)} %copy.65), channel_id=1, source_target_pairs={{8,0},{16,8},{24,16},{32,24},{40,32},{48,40},{56,48},{64,56},{72,6... | collective-permute-start | bytes 196616 | tf_op jit(solution)/shard_map/ppermute | solution.py:23
  26.4 8.8 %copy-start.1 = (f32[32,64,8,8]{0,3,2,1:T(8,128)}, f32[32,64,8,8]{0,3,2,1:T(8,128)S(1)}, u32[]{:S(2)}) copy-start(f32[32,64,8,8]{0,3,2,1:T(8,128)S(1)} %broadcast_in_dim.28) | copy-start | bytes 1572868
  89.8 77.0 %collective-permute-start.2 = (bf16[64,66,1]{1,0,2:T(8,128)(2,1)S(1)}, bf16[64,66,1]{1,0,2:T(8,128)(2,1)S(1)}, u32[]{:S(2)}, u32[]{:S(2)}) collective-permute-start(bf16[64,66,1]{1,0,2:T(8,128)(2,1)S(1)} %get-tuple-element.10), channel_id=1, source_target_pairs={{0,1},{1,2},{2,3},{3,4},{4,5},{5,6},{6,7},{8,9},{9,10},{10,11},{11... | collective-permute-start | bytes 25352 | tf_op jit(solution)/shard_map/ppermute | solution.py:21
  93.0 73.8 %collective-permute-start.3 = (bf16[64,66,1]{1,0,2:T(8,128)(2,1)S(1)}, bf16[64,66,1]{1,0,2:T(8,128)(2,1)S(1)}, u32[]{:S(2)}, u32[]{:S(2)}) collective-permute-start(bf16[64,66,1]{1,0,2:T(8,128)(2,1)S(1)} %get-tuple-element.11), channel_id=1, source_target_pairs={{1,0},{2,1},{3,2},{4,3},{5,4},{6,5},{7,6},{9,8},{10,9},{11,10},{12... | collective-permute-start | bytes 25352 | tf_op jit(solution)/shard_map/ppermute | solution.py:23
  348.3 17.3 %copy-start.2 = (f32[32,64,8,8]{0,3,2,1:T(8,128)S(1)}, f32[32,64,8,8]{0,3,2,1:T(8,128)}, u32[]{:S(2)}) copy-start(f32[32,64,8,8]{0,3,2,1:T(8,128)} %copy-done.1) | copy-start | bytes 1572868
  365.6 10.2 %copy-start = (f32[4096,512]{1,0:T(8,128)S(1)}, f32[4096,512]{1,0:T(8,128)}, u32[]{:S(2)}) copy-start(f32[4096,512]{1,0:T(8,128)} %get-tuple-element.16) | copy-start | bytes 25165828
  365.6 18.0 %copy-start.3 = (f32[32,64,8,8]{0,3,2,1:T(8,128)S(1)}, f32[32,64,8,8]{0,3,2,1:T(8,128)}, u32[]{:S(2)}) copy-start(f32[32,64,8,8]{0,3,2,1:T(8,128)} %broadcast_in_dim.32) | copy-start | bytes 1572868
  383.5 88.8 %copy-start.6 = (f32[32,8,8]{0,2,1:T(8,128)S(1)}, f32[32,8,8]{0,2,1:T(8,128)}, u32[]{:S(2)}) copy-start(f32[32,8,8]{0,2,1:T(8,128)} %convolution_reduce_fusion) | copy-start | bytes 24580
  383.5 88.8 %copy-start.8 = (f32[32]{0:T(128)S(1)}, f32[32]{0:T(128)}, u32[]{:S(2)}) copy-start(f32[32]{0:T(128)} %broadcast_multiply_fusion) | copy-start | bytes 388
Sparse Core Ops, SparseCore 0:
  472.4 131.7 all-reduce.4
where the time goes:
time: 621 us; the launch traced here: 613 us
  other arithmetic  175 us (28%)
  blocking collectives  128 us (21%)
  local copies, waits for them, and re-layouts  106 us (17%)
  waiting for transfers between devices  105 us (17%)
  matrix products  70.4 us (11%)
  between operations  16.1 us (3%)
  starting transfers between devices  12.7 us (2%)
    add x1, other arithmetic, warp_image(): summed = summed + weight_x[along_x] * weight_y[along_y] * partial_z  119 us
    psum x1, waiting for transfers between devices, local(): lax.psum((grad_depth, first_depth, level_sum), 'gy')  105 us
    psum x1, blocking collectives, local(): energy = lax.psum(local_energy, ('gy', 'gz'))  68.7 us
    unnamed x24, local copies, waits for them, and re-layouts  52.3 us
    concatenate x2, other arithmetic, extended(): jnp.concatenate([lax.ppermute(tail, axis, [(i, (i + 1) % count) for i in...  48.1 us
    psum x1, blocking collectives, local(): lax.psum((grad_depth, first_depth, level_sum), 'gy')  32.9 us
    psum x1, blocking collectives, local(): lax.psum((grad_plane, first_diag, depth_level), 'gz')  26.1 us
    dot_general x2, matrix products, contract_rank(): lax.dot_general(left, right, (((0,), (0,)), ((), ())), precision=highest)  26.1 us
  transfers between devices with their start and end apart: 5, of which 1 were waited for; matrix products, arithmetic and copies ran while one was open for 16% of the time, Pallas kernels for 0%

commit v1 on v0

--- a/solution.py
+++ b/solution.py
@@ -129,7 +129,7 @@
     nodes_x = plane_factors.shape[2]
     nodes_y = plane_factors.shape[3] * lax.axis_size("gy")
     full_z = depth_factors.shape[2] * lax.axis_size("gz")
-    energy = lax.psum(local_energy, ("gy", "gz"))
+    energy = lax.psum(lax.psum(local_energy, "gy"), "gz")
     grad_plane, first_diag, depth_level = lax.psum((grad_plane, first_diag, depth_level), "gz")
     diag_plane = jnp.stack(
         [first_diag, jnp.broadcast_to(depth_level[:, None, None], first_diag.shape)]

time: 621 us -> 591 us (0.952)
  blocking collectives: 128 us -> 62.6 us
  waiting for transfers between devices: 105 us -> 140 us
    psum x2 -> x1, blocking collectives: 102 us -> 33.5 us  [local(): energy = lax.psum(lax.psum(local_energy, 'gy'), 'gz')]
    psum x1, waiting for transfers between devices: 105 us -> 140 us  [local(): lax.psum((grad_depth, first_depth, level_sum), 'gy')]
  transfers between devices with their start and end apart: 5 -> 5, of which waited for: 1 -> 1; matrix products, arithmetic and copies ran while one was open for 16% -> 17% of each run, Pallas kernels for 0% -> 0%
where the time goes in v1:
time: 591 us; the launch traced here: 583 us
  other arithmetic  176 us (30%)
  waiting for transfers between devices  140 us (24%)
  local copies, waits for them, and re-layouts  106 us (18%)
  matrix products  70.8 us (12%)
  blocking collectives  62.6 us (11%)
  between operations  15.8 us (3%)
  starting transfers between devices  12.7 us (2%)
    psum x1, waiting for transfers between devices, local(): lax.psum((grad_depth, first_depth, level_sum), 'gy')  140 us
    add x1, other arithmetic, warp_image(): summed = summed + weight_x[along_x] * weight_y[along_y] * partial_z  119 us
    unnamed x24, local copies, waits for them, and re-layouts  52.1 us
    concatenate x2, other arithmetic, extended(): jnp.concatenate([lax.ppermute(tail, axis, [(i, (i + 1) % count) for i in...  48.3 us
    psum x1, blocking collectives, local(): energy = lax.psum(lax.psum(local_energy, 'gy'), 'gz')  33.5 us
    psum x1, blocking collectives, local(): lax.psum((grad_plane, first_diag, depth_level), 'gz')  29.1 us
    dot_general x2, matrix products, contract_rank(): lax.dot_general(left, right, (((0,), (0,)), ((), ())), precision=highest)  26.5 us
    dot_general x3, matrix products, contract_depth(): lax.dot_general(left, right, (((1,), (1,)), ((), ())), precision=highest)  23.1 us
  transfers between devices with their start and end apart: 5, of which 1 were waited for; matrix products, arithmetic and copies ran while one was open for 17% of the time, Pallas kernels for 0%

profile of v1, /device:TPU:7, one launch (start us, length us, event | category | flops | bytes accessed | tf_op | source)
XLA Modules:
  0.0 583.4 jit_solution(9409270871239238468)
XLA Ops:
  7.2 0.0 copy-start.7
  7.2 0.0 copy-start.5
  7.2 0.0 all-reduce.6.cloned.1.call-start
  7.2 1.4 fusion.133
  8.7 6.0 %collective-permute-start = (bf16[64,1,512]{2,0,1:T(8,128)(2,1)S(1)}, bf16[64,1,512]{2,0,1:T(8,128)(2,1)S(1)}, u32[]{:S(2)}, u32[]{:S(2)}) collective-permute-start(bf16[64,1,512]{2,0,1:T(8,128)(2,1)S(1)} %copy.64), channel_id=1, source_target_pairs={{0,8},{8,16},{16,24},{24,32},{32,40},{40,48},{48,56},{56,64},{64,7... | collective-permute-start | bytes 196616 | tf_op jit(solution)/shard_map/ppermute | solution.py:21
  14.7 0.0 copy-start.4
  14.7 2.2 collective-permute-start.1
  16.9 9.0 %fusion.132 = (bf16[1,64,64,512]{3,2,1,0:T(8,128)(2,1)}, bf16[1,64,64,512]{3,2,1,0:T(8,128)(2,1)}, bf16[1,64,64,512]{3,2,1,0:T(8,128)(2,1)}) fusion(bf16[3,64,64,512]{3,2,1,0:T(8,128)(2,1)} %param.7), kind=kLoop, calls=%fused_computation.173 | loop fusion | bytes 25165824 | tf_op jit(solution)/shard_map/slice | solution.py:39
  25.9 0.0 copy-done.7
  25.9 0.0 copy-done.5
  25.9 0.1 fusion.122
  26.1 0.3 broadcast_in_dim.28
  26.4 0.0 copy-start.1
  26.4 8.8 %fusion.124 = f32[4096,512]{1,0:T(8,128)} fusion(f32[32,4096]{0,1:T(8,128)S(1)} %bitcast.293, f32[2,32,512]{2,1,0:T(8,128)S(1)} %copy-done.5), kind=kOutput, calls=%fused_computation.159 | convolution fusion | flops 805306368 | bytes 10551296 | tf_op jit(solution)/shard_map/dot_general | solution.py:67
  35.1 0.0 copy-done.1
  35.2 0.0 copy-done.4
  35.2 1.2 convert_multiply_fusion
  36.4 7.5 %convolution_reduce_fusion = f32[32,8,8]{0,2,1:T(8,128)} fusion(f32[8,8,8,8,512]{4,3,2,1,0:T(8,128)S(1)} %bitcast.291, f32[2,32,512]{2,1,0:T(8,128)S(1)} %copy-done.5), kind=kOutput, calls=%fused_computation.139 | convolution fusion | flops 805451776 | bytes 8462336 | tf_op jit(solution)/shard_map/dot_general | solution.py:75
  43.9 0.3 broadcast_in_dim.34
  44.2 5.7 convolution_bitcast_fusion.2
  49.9 0.6 broadcast_multiply_fusion
  50.4 13.0 %copy.49 = bf16[64,64,512]{1,0,2:T(8,128)(2,1)} copy(bf16[64,64,512]{2,1,0:T(8,128)(2,1)} %param.6) | data formatting | bytes 8388608 | tf_op args[1]
  63.4 0.2 copy.59
  63.6 0.0 collective-permute-done
  63.6 12.7 %copy.48 = bf16[64,1,512]{1,0,2:T(8,128)(2,1)} copy(bf16[64,1,512]{2,0,1:T(8,128)(2,1)S(1)} %collective-permute-done) | data formatting | bytes 131072 | tf_op jit(solution)/shard_map/ppermute | solution.py:21
  76.2 0.0 collective-permute-done.1
  76.2 12.7 %copy.50 = bf16[64,1,512]{1,0,2:T(8,128)(2,1)} copy(bf16[64,1,512]{2,0,1:T(8,128)(2,1)S(1)} %collective-permute-done.1) | data formatting | bytes 131072 | tf_op jit(solution)/shard_map/ppermute | solution.py:23
  88.9 0.9 pad_maximum_fusion.5
  89.8 3.2 collective-permute-start.2
  93.0 1.3 collective-permute-start.3
  94.3 0.3 broadcast_reduce_fusion
  94.7 13.2 %copy.61 = bf16[1,64,64,512]{2,1,3,0:T(8,128)(2,1)} copy(bf16[1,64,64,512]{3,2,1,0:T(8,128)(2,1)} %get-tuple-element.17) | data formatting | bytes 8388608
  107.8 13.0 %copy.62 = bf16[1,64,64,512]{2,1,3,0:T(8,128)(2,1)} copy(bf16[1,64,64,512]{3,2,1,0:T(8,128)(2,1)} %get-tuple-element.16) | data formatting | bytes 8388608
  120.8 12.9 %copy.63 = bf16[1,64,64,512]{2,1,3,0:T(8,128)(2,1)} copy(bf16[1,64,64,512]{3,2,1,0:T(8,128)(2,1)} %get-tuple-element.15) | data formatting | bytes 8388608
  133.7 0.0 collective-permute-done.2
  133.7 0.0 collective-permute-done.3
  133.7 24.1 %maximum_maximum_fusion = (bf16[64,66,513]{1,0,2:T(8,128)(2,1)S(1)}, bf16[64,66,513]{1,0,2:T(8,128)(2,1)}) fusion(bf16[64,1,512]{1,0,2:T(8,128)(2,1)} %copy.50, bf16[64,64,512]{1,0,2:T(8,128)(2,1)} %copy.49, bf16[64,1,512]{1,0,2:T(8,128)(2,1)} %copy.48, bf16[64,66,1]{1,0,2:T(8,128)(2,1)S(1)} %collective-permute-done.2, ...), kind=kLoop, calls=%fused_computation.126 | loop fusion | flops 34670592 | bytes 13009920 | tf_op jit(solution)/shard_map/concatenate | solution.py:19
  157.8 24.2 %select_maximum_fusion = bf16[66,66,514]{1,0,2:T(8,128)(2,1)S(1)} fusion(bf16[64,66,1]{1,0,2:T(8,128)(2,1)S(1)} %collective-permute-done.3, bf16[64,66,1]{1,0,2:T(8,128)(2,1)S(1)} %collective-permute-done.2, bf16[64,1,512]{1,0,2:T(8,128)(2,1)} %copy.50, bf16[64,64,512]{1,0,2:T(8,128)(2,1)} %copy.49, bf16[64,1,512]{1,0,2:T(8,128)(2,1)} %copy.48), kind=kLoop, calls=%fused_computation.119 | loop fusion | flops 40301712 | bytes 8820240 | tf_op jit(solution)/shard_map/concatenate | solution.py:19
  182.1 118.9 %fusion.15 = f32[64,64,512]{1,0,2:T(8,128)} fusion(bf16[1,64,64,512]{2,1,3,0:T(8,128)(2,1)} %copy.61, bf16[1,64,64,512]{2,1,3,0:T(8,128)(2,1)} %copy.62, bf16[1,64,64,512]{2,1,3,0:T(8,128)(2,1)} %copy.63, bf16[64,64,512]{1,0,2:T(8,128)(2,1)} %copy.49, bf16[66,66,514]{1,0,2:T(8,128)(2,1)S(1)} %select_maximum_fusion, ...), kind=kLoop, calls=%fused_computation.26 | loop fusion | flops 293601280 | bytes 125960192 | tf_op jit(solution)/shard_map/add | solution.py:51
  301.0 12.7 %copy.56 = f32[64,64,512]{2,1,0:T(8,128)} copy(f32[64,64,512]{1,0,2:T(8,128)} %fusion.15) | data formatting | bytes 16777216 | tf_op jit(solution)/shard_map/add | solution.py:51
  313.8 1.6 broadcast_in_dim.32
  315.4 17.8 %multiply_reduce_fusion = (f32[]{:T(128)}, f32[4096,512]{1,0:T(8,128)}, bf16[4096,512]{1,0:T(8,128)(2,1)}, f32[4096,512]{1,0:T(8,128)S(1)}) fusion(bf16[64,64,512]{2,1,0:T(8,128)(2,1)} %param.5, f32[32,4096]{0,1:T(8,128)} %bitcast.295, f32[2,32,512]{2,1,0:T(8,128)S(1)} %copy-done.5, f32[4096,512]{1,0:T(8,128)} %fusion.124, f32[64,64,512]{2,1,0:T(8,128)} %copy.56), kind=kOutput, calls=%fused_computation.135 | convolution fusion | flops 822083584 | bytes 42532868 | tf_op jit(solution)/shard_map/dot_general | solution.py:67
  333.2 0.0 copy-done.2
  333.2 10.2 %convolution_bitcast_fusion.4 = f32[1,32,512]{2,1,0:T(8,128)S(1)} fusion(f32[4096,512]{1,0:T(8,128)} %get-tuple-element.19, f32[32,4096]{0,1:T(8,128)S(1)} %bitcast.294), kind=kOutput, calls=%fused_computation.142 | convolution fusion | flops 805306368 | bytes 8978432 | tf_op jit(solution)/shard_map/dot_general | solution.py:71
  343.3 0.0 copy-done
  343.3 7.7 %convolution_bitcast_fusion.1 = f32[32,4096]{1,0:T(8,128)S(1)} fusion(f32[4096,512]{1,0:T(8,128)S(1)} %copy-done, f32[2,32,512]{2,1,0:T(8,128)S(1)} %copy-done.5), kind=kOutput, calls=%fused_computation.137 | convolution fusion | flops 805306368 | bytes 8978432 | tf_op jit(solution)/shard_map/dot_general | solution.py:75
  351.1 0.0 copy-start.6
  351.1 0.0 copy-start.8
  351.1 0.0 copy-done.3
  351.1 5.3 convolution_bitcast_fusion.3
  356.4 7.9 %convolution_bitcast_fusion = f32[32,4096]{1,0:T(8,128)S(1)} fusion(f32[4096,512]{1,0:T(8,128)S(1)} %get-tuple-element.25, f32[2,32,512]{2,1,0:T(8,128)S(1)} %copy-done.5), kind=kOutput, calls=%fused_computation.136 | convolution fusion | flops 805306368 | bytes 8978432 | tf_op jit(solution)/shard_map/dot_general | solution.py:75
  364.3 0.6 copy.57
  364.9 1.9 copy.58
  366.9 2.2 maximum_reduce_fusion
  369.1 33.5 %all-reduce.1 = (f32[]{:T(128)}, f32[32]{0:T(128)S(1)}) all-reduce(f32[]{:T(128)} %get-tuple-element.18, f32[32]{0:T(128)S(1)} %broadcast_reduce_fusion), channel_id=1, replica_groups=mesh['gy'=16,'gz'=8] {'gy'}, use_global_device_ids=true, to_apply=%region_7.8 | all-reduce | flops 33 | bytes 264 | tf_op jit(solution)/shard_map/psum | solution.py:132
  402.6 0.0 copy-done.6
  402.6 0.0 copy-done.8
  402.6 29.1 %all-reduce.3 = (f32[32]{0:T(128)S(1)}, f32[1,32,8,8]{1,3,2,0:T(8,128)S(1)}, f32[2,32,8,8]{1,3,2,0:T(8,128)S(1)}, f32[]{:T(128)}) all-reduce(f32[32]{0:T(128)S(1)} %copy-done.8, f32[1,32,8,8]{1,3,2,0:T(8,128)S(1)} %bitcast.303, f32[2,32,8,8]{1,3,2,0:T(8,128)S(1)} %neg.13, f32[]{:T(128)} %get-tuple-element.3), channel_id=1, replica_groups=mesh['gy'=16,'gz'=8] {'gz'}, use_global_device_ids=true, to_apply=%region_5.6 | all-reduce | flops 6177 | bytes 49416 | tf_op jit(solution)/shard_map/psum | solution.py:133
  433.1 0.7 maximum_negate_fusion
  433.7 0.0 all-reduce.6.cloned.1.call-update
  433.8 0.7 fusion.118
  434.4 140.2 %all-reduce.6.cloned.1.call-done = (f32[1,32,512]{2,1,0:T(8,128)}, f32[2,32,512]{2,1,0:T(8,128)}) async-done(((f32[1,32,512]{2,1,0:T(8,128)}, f32[2,32,512]{2,1,0:T(8,128)}), (f32[1,32,512]{2,1,0:T(8,128)}, f32[2,32,512]{2,1,0:T(8,128)})) %all-reduce.6.cloned.1.call-update) | async-done | bytes 196624 | tf_op jit(solution)/shard_map/psum | solution.py:140
  574.6 0.1 stack_broadcast_in_dim.5
  574.7 1.6 fusion.116
  (11 shorter events, 0.1 us)
Async XLA Ops:
  7.2 18.8 %copy-start.7 = (f32[2,32,8,8]{1,3,2,0:T(8,128)S(1)}, f32[2,32,8,8]{1,3,2,0:T(8,128)}, u32[]{:S(2)}) copy-start(f32[2,32,8,8]{1,3,2,0:T(8,128)} %param.8) | copy-start | bytes 49156
  7.2 18.8 %copy-start.5 = (f32[2,32,512]{2,1,0:T(8,128)S(1)}, f32[2,32,512]{2,1,0:T(8,128)}, u32[]{:S(2)}) copy-start(f32[2,32,512]{2,1,0:T(8,128)} %param.9) | copy-start | bytes 393220
  7.2 567.4 %all-reduce.6.cloned.1.call-start = ((), (), s32[]{:S(2)}) async-start(), calls=%async_computation | async-start | bytes 393216 | tf_op jit(solution)/shard_map/psum | solution.py:140
  8.7 54.9 %collective-permute-start = (bf16[64,1,512]{2,0,1:T(8,128)(2,1)S(1)}, bf16[64,1,512]{2,0,1:T(8,128)(2,1)S(1)}, u32[]{:S(2)}, u32[]{:S(2)}) collective-permute-start(bf16[64,1,512]{2,0,1:T(8,128)(2,1)S(1)} %copy.64), channel_id=1, source_target_pairs={{0,8},{8,16},{16,24},{24,32},{32,40},{40,48},{48,56},{56,64},{64,7... | collective-permute-start | bytes 196616 | tf_op jit(solution)/shard_map/ppermute | solution.py:21
  14.7 20.5 %copy-start.4 = (bf16[64,64,512]{2,1,0:T(8,128)(2,1)S(1)}, bf16[64,64,512]{2,1,0:T(8,128)(2,1)}, u32[]{:S(2)}) copy-start(bf16[64,64,512]{2,1,0:T(8,128)(2,1)} %param.5) | copy-start | bytes 12582916
  14.7 61.5 %collective-permute-start.1 = (bf16[64,1,512]{2,0,1:T(8,128)(2,1)S(1)}, bf16[64,1,512]{2,0,1:T(8,128)(2,1)S(1)}, u32[]{:S(2)}, u32[]{:S(2)}) collective-permute-start(bf16[64,1,512]{2,0,1:T(8,128)(2,1)S(1)} %copy.65), channel_id=1, source_target_pairs={{8,0},{16,8},{24,16},{32,24},{40,32},{48,40},{56,48},{64,56},{72,6... | collective-permute-start | bytes 196616 | tf_op jit(solution)/shard_map/ppermute | solution.py:23
  26.4 8.8 %copy-start.1 = (f32[32,64,8,8]{0,3,2,1:T(8,128)}, f32[32,64,8,8]{0,3,2,1:T(8,128)S(1)}, u32[]{:S(2)}) copy-start(f32[32,64,8,8]{0,3,2,1:T(8,128)S(1)} %broadcast_in_dim.28) | copy-start | bytes 1572868
  89.8 43.9 %collective-permute-start.2 = (bf16[64,66,1]{1,0,2:T(8,128)(2,1)S(1)}, bf16[64,66,1]{1,0,2:T(8,128)(2,1)S(1)}, u32[]{:S(2)}, u32[]{:S(2)}) collective-permute-start(bf16[64,66,1]{1,0,2:T(8,128)(2,1)S(1)} %get-tuple-element.13), channel_id=1, source_target_pairs={{0,1},{1,2},{2,3},{3,4},{4,5},{5,6},{6,7},{8,9},{9,10},{10,11},{11... | collective-permute-start | bytes 25352 | tf_op jit(solution)/shard_map/ppermute | solution.py:21
  93.0 40.7 %collective-permute-start.3 = (bf16[64,66,1]{1,0,2:T(8,128)(2,1)S(1)}, bf16[64,66,1]{1,0,2:T(8,128)(2,1)S(1)}, u32[]{:S(2)}, u32[]{:S(2)}) collective-permute-start(bf16[64,66,1]{1,0,2:T(8,128)(2,1)S(1)} %get-tuple-element.14), channel_id=1, source_target_pairs={{1,0},{2,1},{3,2},{4,3},{5,4},{6,5},{7,6},{9,8},{10,9},{11,10},{12... | collective-permute-start | bytes 25352 | tf_op jit(solution)/shard_map/ppermute | solution.py:23
  315.4 17.8 %copy-start.2 = (f32[32,64,8,8]{0,3,2,1:T(8,128)S(1)}, f32[32,64,8,8]{0,3,2,1:T(8,128)}, u32[]{:S(2)}) copy-start(f32[32,64,8,8]{0,3,2,1:T(8,128)} %copy-done.1) | copy-start | bytes 1572868
  333.2 10.2 %copy-start = (f32[4096,512]{1,0:T(8,128)S(1)}, f32[4096,512]{1,0:T(8,128)}, u32[]{:S(2)}) copy-start(f32[4096,512]{1,0:T(8,128)} %get-tuple-element.19) | copy-start | bytes 25165828
  333.2 17.9 %copy-start.3 = (f32[32,64,8,8]{0,3,2,1:T(8,128)S(1)}, f32[32,64,8,8]{0,3,2,1:T(8,128)}, u32[]{:S(2)}) copy-start(f32[32,64,8,8]{0,3,2,1:T(8,128)} %broadcast_in_dim.32) | copy-start | bytes 1572868
  351.1 51.6 %copy-start.6 = (f32[32,8,8]{0,2,1:T(8,128)S(1)}, f32[32,8,8]{0,2,1:T(8,128)}, u32[]{:S(2)}) copy-start(f32[32,8,8]{0,2,1:T(8,128)} %convolution_reduce_fusion) | copy-start | bytes 24580
  351.1 51.5 %copy-start.8 = (f32[32]{0:T(128)S(1)}, f32[32]{0:T(128)}, u32[]{:S(2)}) copy-start(f32[32]{0:T(128)} %broadcast_multiply_fusion) | copy-start | bytes 388
Sparse Core Ops, SparseCore 0:
  433.9 140.6 all-reduce.5
